TPU v7x, 32 devices: a whole 2x2x4 slice. The times are simulated.
32 devices in a mesh: dp: 4 (over z), expert: 2 (over x), tensor: 4 (over y, core).
Axes of the slice: x: 2, y: 2, z: 4, core: 2. Of those that a mesh axis runs over, the one named last changes fastest.
Arguments:
- tokens: bfloat16 [128, 4096], P(('dp', 'expert', 'tensor')), may hold values from -6 to 6
- routes: int32 [128, 2], P(('dp', 'expert', 'tensor')), may hold values from 0 to 7, all different within a row; in each aligned block of 4 rows (0 to 3, 4 to 7, ...) at most 2 rows name the same one
- gates: float32 [128, 2], P(('dp', 'expert', 'tensor')), may hold values from 0.1 to 1
- d_out: bfloat16 [128, 4096], P(('dp', 'expert', 'tensor')), may hold values from -3 to 3
- w_in: bfloat16 [8, 2, 7168, 4096], P('expert', None, ('dp', 'tensor')), may hold values from -0.09375 to 0.09375
- w_out: bfloat16 [8, 7168, 4096], P('expert', ('dp', 'tensor')), may hold values from -0.0625 to 0.0625
Outputs:
- mixed: bfloat16 [128, 4096], P(('dp', 'expert', 'tensor'))
- d_tokens: bfloat16 [128, 4096], P(('dp', 'expert', 'tensor'))
- d_gates: float32 [128, 2], P(('dp', 'expert', 'tensor'))
- grad_in: bfloat16 [8, 2, 7168, 4096], P('expert', None, ('dp', 'tensor'))
- grad_out: bfloat16 [8, 7168, 4096], P('expert', ('dp', 'tensor'))
Inputs may be any that keep to these rules, and one draw needn't show every extreme that they name: `routes`: each token names 2 different experts; among the 4 tokens of one device no expert is named more than 2 times, a bound that some block reaches.
All inputs are finite; a program needn't handle non-finite values.
Results may differ from a plain program's by a relative error of at most 0.0065.
Values may be sent and summed in bfloat16 or wider, within the bound.
No kernel may reach another device: no remote copies, remote signals or barrier semaphores. Data moves between devices by JAX's collectives and lax.ppermute only.
A program may use at most 192 MiB of HBM per device.

v0:
```python
import jax
import jax.numpy as jnp
from jax import lax
from jax.sharding import PartitionSpec as P

CAP = 2


def to_groups(buffer, owners, local_experts):
    width = buffer.shape[-1]
    shaped = buffer.reshape(owners, local_experts, CAP, width)
    return jnp.swapaxes(shaped, 0, 1).reshape(local_experts, owners * CAP, width)


def to_owners(summed, owners, local_experts):
    width = summed.shape[-1]
    shaped = summed.astype(jnp.bfloat16).reshape(local_experts, owners, CAP, width)
    return jnp.swapaxes(shaped, 0, 1).reshape(owners, local_experts * CAP, width)


def per_device(tokens, routes, gates, d_out, w_in, w_out):
    tok_count, width = tokens.shape
    top_k = routes.shape[1]
    owners = lax.axis_size("expert")
    local_experts = w_in.shape[0]
    experts_all = owners * local_experts
    flat_routes = routes.reshape(-1)
    one_hot = (flat_routes[:, None] == jnp.arange(experts_all, dtype=jnp.int32)[None, :]).astype(
        jnp.int32
    )
    earlier = jnp.cumsum(one_hot, axis=0) - one_hot
    slot_index = jnp.sum(earlier * one_hot, axis=1)
    target = flat_routes * CAP + slot_index
    placement = (jnp.arange(experts_all * CAP, dtype=jnp.int32)[:, None] == target[None, :]).astype(
        jnp.bfloat16
    )
    token_rows = jnp.repeat(tokens, top_k, axis=0)
    scaled = (gates.reshape(-1, 1) * jnp.repeat(d_out, top_k, axis=0).astype(jnp.float32)).astype(
        jnp.bfloat16
    )
    send_x = jnp.dot(placement, token_rows, preferred_element_type=jnp.float32).astype(jnp.bfloat16)
    send_g = jnp.dot(placement, scaled, preferred_element_type=jnp.float32).astype(jnp.bfloat16)
    send_x = send_x.reshape(owners, local_experts * CAP, width)
    send_g = send_g.reshape(owners, local_experts * CAP, width)
    got_x, got_g = (
        lax.all_to_all(send_x, "expert", split_axis=0, concat_axis=0, tiled=True),
        lax.all_to_all(send_g, "expert", split_axis=0, concat_axis=0, tiled=True),
    )
    rows_x, rows_g = (
        lax.all_gather(
            to_groups(got_x, owners, local_experts), ("dp", "tensor"), axis=1, tiled=True
        ),
        lax.all_gather(
            to_groups(got_g, owners, local_experts), ("dp", "tensor"), axis=1, tiled=True
        ),
    )
    both_pre = jnp.einsum("lrd,lkfd->lkrf", rows_x, w_in, preferred_element_type=jnp.float32)
    gate_pre = both_pre[:, 0]
    up_pre = both_pre[:, 1]
    sigma = jax.nn.sigmoid(gate_pre)
    hidden = (gate_pre * sigma * up_pre).astype(jnp.bfloat16)
    out_terms = jnp.einsum("lrf,lfd->lrd", hidden, w_out, preferred_element_type=jnp.float32)
    out_sum = lax.psum_scatter(out_terms, ("dp", "tensor"), scatter_dimension=1, tiled=True)
    out_back = lax.all_to_all(
        to_owners(out_sum, owners, local_experts), "expert", split_axis=0, concat_axis=0, tiled=True
    )
    d_hidden = jnp.einsum("lrd,lfd->lrf", rows_g, w_out, preferred_element_type=jnp.float32)
    d_gate = d_hidden * up_pre * sigma * (1.0 + gate_pre * (1.0 - sigma))
    d_up = d_hidden * gate_pre * sigma
    d_pre = jnp.stack([d_gate, d_up], axis=1).astype(jnp.bfloat16)
    dx_terms = jnp.einsum("lkrf,lkfd->lrd", d_pre, w_in, preferred_element_type=jnp.float32)
    grad_out = jnp.einsum(
        "lrf,lrd->lfd", hidden, rows_g, preferred_element_type=jnp.float32
    ).astype(jnp.bfloat16)
    grad_in = jnp.einsum(
        "lkrf,lrd->lkfd", d_pre, rows_x, preferred_element_type=jnp.float32
    ).astype(jnp.bfloat16)
    dx_sum = lax.psum_scatter(dx_terms, ("dp", "tensor"), scatter_dimension=1, tiled=True)
    dx_back = lax.all_to_all(
        to_owners(dx_sum, owners, local_experts), "expert", split_axis=0, concat_axis=0, tiled=True
    )
    out_buffer = out_back.reshape(experts_all * CAP, width)
    dx_buffer = dx_back.reshape(experts_all * CAP, width)
    out_route = jnp.einsum(
        "pj,pd->jd", placement, out_buffer, preferred_element_type=jnp.float32
    ).reshape(tok_count, top_k, width)
    dx_route = jnp.einsum(
        "pj,pd->jd", placement, dx_buffer, preferred_element_type=jnp.float32
    ).reshape(tok_count, top_k, width)
    mixed = jnp.sum(gates[:, :, None] * out_route, axis=1).astype(jnp.bfloat16)
    d_tokens = jnp.sum(dx_route, axis=1).astype(jnp.bfloat16)
    d_gates = jnp.sum(d_out.astype(jnp.float32)[:, None, :] * out_route, axis=2)
    return (mixed, d_tokens, d_gates, grad_in, grad_out)


def solution(mesh):
    return jax.shard_map(
        per_device,
        mesh=mesh,
        in_specs=(
            P(("dp", "expert", "tensor"), None),
            P(("dp", "expert", "tensor"), None),
            P(("dp", "expert", "tensor"), None),
            P(("dp", "expert", "tensor"), None),
            P("expert", None, ("dp", "tensor"), None),
            P("expert", ("dp", "tensor"), None),
        ),
        out_specs=(
            P(("dp", "expert", "tensor"), None),
            P(("dp", "expert", "tensor"), None),
            P(("dp", "expert", "tensor"), None),
            P("expert", None, ("dp", "tensor"), None),
            P("expert", ("dp", "tensor"), None),
        ),
        check_vma=False,
    )
```

profile of v0, /device:TPU:1, one launch (start us, length us, event | category | flops | bytes accessed | tf_op | source)
XLA Modules:
  0.0 361.7 jit_solution(2922438015457980727)
XLA Ops:
  7.2 0.0 all-gather.3.cloned.1.call-start
  7.2 0.8 copy.52
  8.0 0.1 reshape.107
  8.1 0.1 fusion.25
  8.2 0.2 select_reduce_fusion
  8.4 0.8 broadcast_in_dim.4
  9.2 0.2 fusion.5
  9.4 6.4 %all_to_all.20 = bf16[2,8,4096]{2,1,0:T(8,128)(2,1)S(1)} all-to-all(bf16[2,8,4096]{2,1,0:T(8,128)(2,1)S(1)} %fusion.5), channel_id=1, replica_groups=mesh['dp'=4,'expert'=2,'tensor'=4] {'expert'}, dimensions={0} | all-to-all | bytes 262144 | tf_op jit(solution)/shard_map/all_to_all | solution.py:46
  15.8 0.1 reshape.110
  15.9 0.8 copy.53
  16.6 0.0 all-gather.3.cloned.1.call-update
  16.7 0.0 all-gather.5.cloned.1.call-start
  16.7 0.8 broadcast_in_dim.5.clone
  17.5 0.1 convert_element_type.49
  17.6 0.8 copy.59
  18.4 0.1 mul.64
  18.5 0.2 fusion.6
  18.7 5.7 %all_to_all.21 = bf16[2,8,4096]{2,1,0:T(8,128)(2,1)S(1)} all-to-all(bf16[2,8,4096]{2,1,0:T(8,128)(2,1)S(1)} %fusion.6), channel_id=1, replica_groups=mesh['dp'=4,'expert'=2,'tensor'=4] {'expert'}, dimensions={0} | all-to-all | bytes 262144 | tf_op jit(solution)/shard_map/all_to_all | solution.py:47
  24.4 0.1 reshape.116
  24.5 0.8 copy.61
  25.3 0.0 all-gather.5.cloned.1.call-update
  25.3 0.8 convert_element_type.48
  26.1 0.1 iota_compare_fusion.4
  26.2 1.2 dynamic-slice
  28.1 32.3 %all-gather.3.cloned.1.call-done = bf16[4,64,4096]{2,0,1:T(4,128)(2,1)} async-done(((bf16[4,4,4096]{2,0,1:T(4,128)(2,1)}), bf16[4,64,4096]{2,0,1:T(4,128)(2,1)}) %all-gather.3.cloned.1.call-update) | async-done | bytes 2097168 | tf_op jit(solution)/shard_map/all_gather | solution.py:50
  60.4 14.6 %fusion.13 = f32[4,2,64,448]{3,2,1,0:T(8,128)S(1)} fusion(bf16[4,2,448,4096]{3,2,1,0:T(8,128)(2,1)} %param.10, bf16[4,64,4096,1]{2,0,1,3:T(4,128)(2,1)} %bitcast.71), kind=kOutput, calls=%fused_computation.15 | convolution fusion | flops 1879048192 | bytes 32374784 | tf_op jit(solution)/shard_map/lrd,lkfd->lkrf/dot_general | solution.py:57
  75.0 28.4 %all-gather.5.cloned.1.call-done = bf16[4,64,4096]{2,0,1:T(4,128)(2,1)} async-done(((bf16[4,4,4096]{2,0,1:T(4,128)(2,1)}), bf16[4,64,4096]{2,0,1:T(4,128)(2,1)}) %all-gather.5.cloned.1.call-update) | async-done | bytes 2097168 | tf_op jit(solution)/shard_map/all_gather | solution.py:53
  103.4 10.4 %fusion.18 = (bf16[4,1,64,448]{3,2,0,1:T(8,128)(2,1)S(1)}, bf16[4,1,64,448]{3,2,0,1:T(8,128)(2,1)S(1)}, bf16[4,64,448]{2,1,0:T(8,128)(2,1)S(1)}) fusion(f32[4,2,64,448]{3,2,1,0:T(8,128)S(1)} %fusion.13, bf16[4,448,4096]{2,1,0:T(8,128)(2,1)} %param.11, bf16[4,64,4096]{2,0,1:T(4,128)(2,1)} %all-gather.5.cloned.1.call-done), kind=kOutput, calls=%fused_computation.28 | convolution fusion | flops 941359104 | bytes 18382848 | tf_op jit(solution)/shard_map/lrd,lfd->lrf/dot_general | solution.py:67
  113.7 0.0 copy-start.1
  113.7 14.2 %fusion.2 = f32[4,64,4096]{2,1,0:T(8,128)} fusion(bf16[4,2,448,4096]{3,2,1,0:T(8,128)(2,1)} %param.10, bf16[4,1,64,448]{3,2,0,1:T(8,128)(2,1)S(1)} %get-tuple-element.10, bf16[4,1,64,448]{3,2,0,1:T(8,128)(2,1)S(1)} %get-tuple-element.9), kind=kOutput, calls=%fused_computation.4 | convolution fusion | flops 1879277568 | bytes 34013184 | tf_op jit(solution)/shard_map/lkrf,lkfd->lrd/dot_general | solution.py:71
  128.0 12.8 %convolution_convert_fusion = bf16[4,2,448,4096]{3,2,1,0:T(8,128)(2,1)} fusion(bf16[4,64,4096,1]{2,0,1,3:T(4,128)(2,1)S(1)} %bitcast.72, bf16[4,1,64,448]{3,2,0,1:T(8,128)(2,1)S(1)} %get-tuple-element.10, bf16[4,1,64,448]{3,2,0,1:T(8,128)(2,1)S(1)} %get-tuple-element.9), kind=kOutput, calls=%fused_computation.2 | convolution fusion | flops 1893957632 | bytes 31916032 | tf_op jit(solution)/shard_map/lkrf,lrd->lkfd/dot_general | solution.py:75
  140.8 9.8 %fusion.30 = f32[4,64,4096]{2,1,0:T(8,128)} fusion(bf16[4,64,448]{2,1,0:T(8,128)(2,1)S(1)} %get-tuple-element.11, bf16[4,448,4096]{2,1,0:T(8,128)(2,1)} %param.11), kind=kOutput, calls=%fused_computation.46 | convolution fusion | flops 939524096 | bytes 19103744 | tf_op jit(solution)/shard_map/lrf,lfd->lrd/dot_general | solution.py:62
  150.6 182.6 %all-reduce.4 = (bf16[4,64,4096]{2,1,0:T(8,128)(2,1)}, bf16[4,64,4096]{2,1,0:T(8,128)(2,1)}) all-reduce(f32[4,64,4096]{2,1,0:T(8,128)} %fusion.30, f32[4,64,4096]{2,1,0:T(8,128)} %fusion.2), channel_id=2, replica_groups=mesh['dp'=4,'expert'=2,'tensor'=4] {'dp','tensor'}, use_global_device_ids=true, to_apply=%region_2.3.clone | all-reduce | flops 2097152 | bytes 12582912
  333.2 1.2 dynamic-slice_convert_fusion
  334.3 0.1 reshape.118
  334.4 0.1 copy.64
  334.6 0.7 copy.65
  335.3 3.4 all-to-all-start.3
  338.7 0.0 copy-start.2
  338.7 7.6 %convolution_convert_fusion.1 = bf16[4,448,4096]{2,1,0:T(8,128)(2,1)} fusion(bf16[4,64,448]{2,1,0:T(8,128)(2,1)S(1)} %get-tuple-element.11, bf16[4,64,4096]{2,0,1:T(4,128)(2,1)S(1)} %copy-done), kind=kOutput, calls=%fused_computation.3 | convolution fusion | flops 946864128 | bytes 17006592 | tf_op jit(solution)/shard_map/lrf,lrd->lfd/dot_general | solution.py:72
  346.3 0.1 reshape.112
  346.4 0.1 copy.56
  346.5 0.7 copy.57
  347.3 0.0 all-to-all-done.3
  347.3 3.4 all-to-all-start.1
  350.7 0.8 convolution_reduce_fusion
  351.5 2.5 all-to-all-done.1
  354.0 0.9 multiply_reduce_fusion
  (8 shorter events, 0.1 us)
Async XLA Ops:
  7.2 53.2 %all-gather.3.cloned.1.call-start = ((), (), s32[]{:S(2)}) async-start(), calls=%async_computation.4 | async-start | bytes 2228224 | tf_op jit(solution)/shard_map/all_gather | solution.py:50
  16.7 86.7 %all-gather.5.cloned.1.call-start = ((), (), s32[]{:S(2)}) async-start(), calls=%async_computation.5 | async-start | bytes 2228224 | tf_op jit(solution)/shard_map/all_gather | solution.py:53
  113.7 14.3 %copy-start.1 = (bf16[4,64,4096]{2,0,1:T(4,128)(2,1)S(1)}, bf16[4,64,4096]{2,0,1:T(4,128)(2,1)}, u32[]{:S(2)}) copy-start(bf16[4,64,4096]{2,0,1:T(4,128)(2,1)} %all-gather.3.cloned.1.call-done) | copy-start | bytes 6291460
  150.6 188.1 %copy-start = (bf16[4,64,4096]{2,0,1:T(4,128)(2,1)S(1)}, bf16[4,64,4096]{2,0,1:T(4,128)(2,1)}, u32[]{:S(2)}) copy-start(bf16[4,64,4096]{2,0,1:T(4,128)(2,1)} %all-gather.5.cloned.1.call-done) | copy-start | bytes 6291460
  335.3 12.0 %all-to-all-start.3 = ((bf16[2,8,4096]{2,1,0:T(8,128)(2,1)}), bf16[2,8,4096]{2,1,0:T(8,128)(2,1)S(1)}, u32[]{:S(2)}, u32[]{:S(2)}) async-start(bf16[2,8,4096]{2,1,0:T(8,128)(2,1)} %copy.65), calls=%async_computation.3 | async-start | bytes 262144 | tf_op jit(solution)/shard_map/all_to_all | solution.py:79
  338.7 15.3 %copy-start.2 = (f32[4,2]{0,1:T(2,128)S(1)}, f32[4,2]{0,1:T(2,128)}, u32[]{:S(2)}) copy-start(f32[4,2]{0,1:T(2,128)} %param.8) | copy-start | bytes 100
  347.3 6.7 %all-to-all-start.1 = ((bf16[2,8,4096]{2,1,0:T(8,128)(2,1)}), bf16[2,8,4096]{2,1,0:T(8,128)(2,1)S(1)}, u32[]{:S(2)}, u32[]{:S(2)}) async-start(bf16[2,8,4096]{2,1,0:T(8,128)(2,1)} %copy.57), calls=%async_computation.1 | async-start | bytes 262144 | tf_op jit(solution)/shard_map/all_to_all | solution.py:64
Sparse Core Ops, SparseCore 0:
  16.8 43.5 all-gather.2
  63.1 40.1 all-gather.4
where the time goes:
time: 362 us
  blocking collectives  195 us (54%)
  matrix products  71.5 us (20%)
  waiting for transfers between devices  63.3 us (17%)
  between operations  14.8 us (4%)
  local copies, waits for them, and re-layouts  9.46 us (3%)
  starting transfers between devices  6.83 us (2%)
    unnamed x1, blocking collectives  183 us
    all_gather x1, waiting for transfers between devices, per_device(): lax.all_gather(to_groups(got_x, owners, local_experts), ('dp', 'tensor'),...  32.3 us
    all_gather x1, waiting for transfers between devices, per_device(): lax.all_gather(to_groups(got_g, owners, local_experts), ('dp', 'tensor'),...  28.4 us
    dot_general x1, matrix products, per_device(): jnp.einsum('lrd,lkfd->lkrf', rows_x, w_in, preferred_element_type=jnp.flo...  14.6 us
    dot_general x1, matrix products, per_device(): jnp.einsum('lkrf,lkfd->lrd', d_pre, w_in, preferred_element_type=jnp.floa...  14.2 us
    dot_general x1, matrix products, per_device(): jnp.einsum('lkrf,lrd->lkfd', d_pre, rows_x, preferred_element_type=jnp.fl...  12.8 us
    dot_general x1, matrix products, per_device(): jnp.einsum('lrd,lfd->lrf', rows_g, w_out, preferred_element_type=jnp.floa...  10.4 us
    dot_general x1, matrix products, per_device(): jnp.einsum('lrf,lfd->lrd', hidden, w_out, preferred_element_type=jnp.floa...  9.81 us
  transfers between devices with their start and end apart: 4, of which 3 were waited for; matrix products, arithmetic and copies ran while one was open for 8% of the time, Pallas kernels for 0%

commit v1 on v0

--- a/solution.py
+++ b/solution.py
@@ -50,8 +50,16 @@
         lax.all_gather(
             to_groups(got_x, owners, local_experts), ("dp", "tensor"), axis=1, tiled=True
         ),
-        lax.all_gather(
-            to_groups(got_g, owners, local_experts), ("dp", "tensor"), axis=1, tiled=True
+        jnp.concatenate(
+            lax.all_to_all(
+                jnp.stack(
+                    [to_groups(got_g, owners, local_experts)] * lax.axis_size(("dp", "tensor"))
+                ),
+                ("dp", "tensor"),
+                0,
+                0,
+            ),
+            axis=1,
         ),
     )
     both_pre = jnp.einsum("lrd,lkfd->lkrf", rows_x, w_in, preferred_element_type=jnp.float32)

time: 362 us -> 377 us (1.041); the launches traced: 362 us -> 372 us
  starting transfers between devices: 6.83 us -> 22.6 us
  blocking collectives: 195 us -> 184 us
  local copies, waits for them, and re-layouts: 9.46 us -> 15.4 us
    all_to_all x0 -> x3, waiting for transfers between devices: none -> 48.6 us  [the longest x1 43.5 us: per_device(): lax.all_to_all(jnp.stack([to_groups(got_g, owners, local_experts)] * lax....]
    all_gather x1 -> x0, waiting for transfers between devices: 28.4 us -> none  [per_device(): lax.all_gather(to_groups(got_g, owners, local_experts), ('dp', 'tensor'),...]
    all_gather x1, waiting for transfers between devices: 32.3 us -> 10.5 us  [per_device(): lax.all_gather(to_groups(got_x, owners, local_experts), ('dp', 'tensor'),...]
    all_to_all x0 -> x3, starting transfers between devices: none -> 15.8 us  [the longest x1 9.07 us: per_device(): lax.all_to_all(jnp.stack([to_groups(got_g, owners, local_experts)] * lax....]
    all_to_all x2 -> x0, blocking collectives: 12.1 us -> none  [the longest x1 6.42 us: per_device(): lax.all_to_all(send_x, 'expert', split_axis=0, concat_axis=0, tiled=True)]
    reshape x0 -> x2, local copies, waits for them, and re-layouts: none -> 4.78 us  [per_device(): jnp.concatenate(lax.all_to_all(jnp.stack([to_groups(got_g, owners, local_...]
  transfers between devices with their start and end apart: 4 -> 6, of which waited for: 3 -> 5; matrix products, arithmetic and copies ran while one was open for 8% -> 5% of each run, Pallas kernels for 0% -> 0%
where the time goes in v1:
time: 377 us; the launch traced here: 372 us
  blocking collectives  184 us (49%)
  matrix products  71.9 us (19%)
  waiting for transfers between devices  62.4 us (17%)
  starting transfers between devices  22.6 us (6%)
  local copies, waits for them, and re-layouts  15.4 us (4%)
  between operations  14.9 us (4%)
    unnamed x1, blocking collectives  184 us
    all_to_all x1, waiting for transfers between devices, per_device(): lax.all_to_all(jnp.stack([to_groups(got_g, owners, local_experts)] * lax....  43.5 us
    dot_general x1, matrix products, per_device(): jnp.einsum('lrd,lkfd->lkrf', rows_x, w_in, preferred_element_type=jnp.flo...  14.5 us
    dot_general x1, matrix products, per_device(): jnp.einsum('lkrf,lkfd->lrd', d_pre, w_in, preferred_element_type=jnp.floa...  14.3 us
    dot_general x1, matrix products, per_device(): jnp.einsum('lkrf,lrd->lkfd', d_pre, rows_x, preferred_element_type=jnp.fl...  12.8 us
    all_gather x1, waiting for transfers between devices, per_device(): lax.all_gather(to_groups(got_x, owners, local_experts), ('dp', 'tensor'),...  10.5 us
    dot_general x1, matrix products, per_device(): jnp.einsum('lrf,lfd->lrd', hidden, w_out, preferred_element_type=jnp.floa...  9.81 us
    dot_general x1, matrix products, per_device(): jnp.einsum('lrd,lfd->lrf', rows_g, w_out, preferred_element_type=jnp.floa...  9.55 us
  transfers between devices with their start and end apart: 6, of which 5 were waited for; matrix products, arithmetic and copies ran while one was open for 5% of the time, Pallas kernels for 0%

profile of v1, /device:TPU:1, one launch (start us, length us, event | category | flops | bytes accessed | tf_op | source)
XLA Modules:
  0.0 371.7 jit_solution(1510624947984279419)
XLA Ops:
  7.2 0.8 copy.68
  7.9 0.1 reshape.112
  8.0 0.1 fusion.22
  8.1 0.2 select_reduce_fusion
  8.3 0.8 broadcast_in_dim.5.clone
  9.1 0.1 convert_element_type.49
  9.2 0.8 copy.75
  10.0 0.1 mul.64
  10.1 0.9 fusion.6
  11.0 3.4 all-to-all-start.2
  14.3 0.8 broadcast_in_dim.4
  15.2 0.8 fusion.5
  16.0 2.2 all-to-all-done.2
  18.2 3.4 all-to-all-start
  21.6 0.1 copy.77
  21.7 0.1 copy.78
  21.9 0.1 copy.79
  22.0 2.9 all-to-all-done
  24.9 2.3 stack.15
  27.2 9.1 %all-to-all-start.3 = ((bf16[16,4,4,4096]{3,2,1,0:T(4,128)(2,1)}), bf16[16,4,4,4096]{3,2,1,0:T(4,128)(2,1)S(1)}, u32[]{:S(2)}, u32[]{:S(2)}) async-start(bf16[16,4,4,4096]{3,2,1,0:T(4,128)(2,1)} %stack.15), calls=%async_computation.3 | async-start | bytes 4194304 | tf_op jit(solution)/shard_map/all_to_all | solution.py:54
  36.3 0.0 all-gather.2.cloned.1.call-start
  36.4 0.1 reshape.115
  36.5 0.8 copy.69
  37.3 0.1 iota_compare_fusion.4
  37.4 0.6 dynamic-slice
  38.6 43.5 %all-to-all-done.3 = bf16[16,4,4,4096]{3,2,1,0:T(4,128)(2,1)S(1)} async-done(((bf16[16,4,4,4096]{3,2,1,0:T(4,128)(2,1)}), bf16[16,4,4,4096]{3,2,1,0:T(4,128)(2,1)S(1)}, u32[]{:S(2)}, u32[]{:S(2)}) %all-to-all-start.3) | async-done | bytes 2097184 | tf_op jit(solution)/shard_map/all_to_all | solution.py:54
  82.1 2.2 copy.80
  84.4 2.5 reshape.123
  86.9 10.5 %all-gather.2.cloned.1.call-done = bf16[4,64,4096]{2,0,1:T(4,128)(2,1)} async-done(((bf16[4,4,4096]{2,0,1:T(4,128)(2,1)}), bf16[4,64,4096]{2,0,1:T(4,128)(2,1)}) %all-gather.2.cloned.1.call-update) | async-done | bytes 2097168 | tf_op jit(solution)/shard_map/all_gather | solution.py:50
  97.4 14.5 %fusion.10 = f32[4,2,64,448]{3,2,1,0:T(8,128)S(1)} fusion(bf16[4,2,448,4096]{3,2,1,0:T(8,128)(2,1)} %param.10, bf16[4,64,4096,1]{2,0,1,3:T(4,128)(2,1)} %bitcast.76), kind=kOutput, calls=%fused_computation.12 | convolution fusion | flops 1879048192 | bytes 32374784 | tf_op jit(solution)/shard_map/lrd,lkfd->lkrf/dot_general | solution.py:65
  111.9 9.5 %fusion.15 = (bf16[4,1,64,448]{3,2,0,1:T(8,128)(2,1)S(1)}, bf16[4,1,64,448]{3,2,0,1:T(8,128)(2,1)S(1)}, bf16[4,64,448]{2,1,0:T(8,128)(2,1)S(1)}) fusion(f32[4,2,64,448]{3,2,1,0:T(8,128)S(1)} %fusion.10, bf16[4,64,4096]{2,1,0:T(8,128)(2,1)S(1)} %reshape.123, bf16[4,448,4096]{2,1,0:T(8,128)(2,1)} %param.11), kind=kOutput, calls=%fused_computation.25 | convolution fusion | flops 941359104 | bytes 18382848 | tf_op jit(solution)/shard_map/lrd,lfd->lrf/dot_general | solution.py:75
  121.5 14.3 %fusion.2 = f32[4,64,4096]{2,1,0:T(8,128)} fusion(bf16[4,2,448,4096]{3,2,1,0:T(8,128)(2,1)} %param.10, bf16[4,1,64,448]{3,2,0,1:T(8,128)(2,1)S(1)} %get-tuple-element.10, bf16[4,1,64,448]{3,2,0,1:T(8,128)(2,1)S(1)} %get-tuple-element.9), kind=kOutput, calls=%fused_computation.4 | convolution fusion | flops 1879277568 | bytes 34013184 | tf_op jit(solution)/shard_map/lkrf,lkfd->lrd/dot_general | solution.py:79
  135.8 12.8 %convolution_convert_fusion = bf16[4,2,448,4096]{3,2,1,0:T(8,128)(2,1)} fusion(bf16[4,64,4096,1]{2,0,1,3:T(4,128)(2,1)S(1)} %bitcast.77, bf16[4,1,64,448]{3,2,0,1:T(8,128)(2,1)S(1)} %get-tuple-element.10, bf16[4,1,64,448]{3,2,0,1:T(8,128)(2,1)S(1)} %get-tuple-element.9), kind=kOutput, calls=%fused_computation.2 | convolution fusion | flops 1893957632 | bytes 31916032 | tf_op jit(solution)/shard_map/lkrf,lrd->lkfd/dot_general | solution.py:83
  148.6 9.8 %fusion.25 = f32[4,64,4096]{2,1,0:T(8,128)} fusion(bf16[4,64,448]{2,1,0:T(8,128)(2,1)S(1)} %get-tuple-element.11, bf16[4,448,4096]{2,1,0:T(8,128)(2,1)} %param.11), kind=kOutput, calls=%fused_computation.43 | convolution fusion | flops 939524096 | bytes 19103744 | tf_op jit(solution)/shard_map/lrf,lfd->lrd/dot_general | solution.py:70
  158.4 184.1 %all-reduce.4 = (bf16[4,64,4096]{2,1,0:T(8,128)(2,1)}, bf16[4,64,4096]{2,1,0:T(8,128)(2,1)}) all-reduce(f32[4,64,4096]{2,1,0:T(8,128)} %fusion.25, f32[4,64,4096]{2,1,0:T(8,128)} %fusion.2), channel_id=2, replica_groups=mesh['dp'=4,'expert'=2,'tensor'=4] {'dp','tensor'}, use_global_device_ids=true, to_apply=%region_2.3.clone | all-reduce | flops 2097152 | bytes 12582912
  342.4 1.2 dynamic-slice_convert_fusion
  343.6 0.1 reshape.124
  343.7 0.1 copy.82
  343.8 0.7 copy.83
  344.5 3.4 all-to-all-start.4
  347.9 7.6 %convolution_convert_fusion.1 = bf16[4,448,4096]{2,1,0:T(8,128)(2,1)} fusion(bf16[4,64,448]{2,1,0:T(8,128)(2,1)S(1)} %get-tuple-element.11, bf16[4,64,4096]{2,1,0:T(8,128)(2,1)S(1)} %reshape.123), kind=kOutput, calls=%fused_computation.3 | convolution fusion | flops 946864128 | bytes 17006592 | tf_op jit(solution)/shard_map/lrf,lrd->lfd/dot_general | solution.py:80
  355.5 0.1 reshape.117
  355.6 0.1 copy.72
  355.7 0.7 copy.73
  356.5 3.4 all-to-all-start.1
  359.9 0.8 convolution_reduce_fusion
  360.6 3.3 all-to-all-done.1
  363.9 0.9 multiply_reduce_fusion
  (15 shorter events, 0.1 us)
Async XLA Ops:
  11.0 7.3 %all-to-all-start.2 = ((bf16[2,8,4096]{2,1,0:T(8,128)(2,1)}), bf16[2,8,4096]{2,1,0:T(8,128)(2,1)S(1)}, u32[]{:S(2)}, u32[]{:S(2)}) async-start(bf16[2,8,4096]{2,1,0:T(8,128)(2,1)} %fusion.6), calls=%async_computation.2 | async-start | bytes 262144 | tf_op jit(solution)/shard_map/all_to_all | solution.py:47
  15.2 22.1 %copy-start.1 = (bf16[4,4096]{1,0:T(4,128)(2,1)S(1)}, bf16[4,4096]{1,0:T(4,128)(2,1)}, u32[]{:S(2)}) copy-start(bf16[4,4096]{1,0:T(4,128)(2,1)} %param.9) | copy-start | bytes 98308
  15.2 22.2 %copy-start.3 = (u32[32]{0:T(128)S(1)}, u32[32]{0:T(128)}, u32[]{:S(2)}) copy-start(u32[32]{0:T(128)} %constant.18) | copy-start | bytes 388
  18.2 6.7 %all-to-all-start = ((bf16[2,8,4096]{2,1,0:T(8,128)(2,1)}), bf16[2,8,4096]{2,1,0:T(8,128)(2,1)S(1)}, u32[]{:S(2)}, u32[]{:S(2)}) async-start(bf16[2,8,4096]{2,1,0:T(8,128)(2,1)} %fusion.5), calls=%async_computation | async-start | bytes 262144 | tf_op jit(solution)/shard_map/all_to_all | solution.py:46
  27.2 54.9 %all-to-all-start.3 = ((bf16[16,4,4,4096]{3,2,1,0:T(4,128)(2,1)}), bf16[16,4,4,4096]{3,2,1,0:T(4,128)(2,1)S(1)}, u32[]{:S(2)}, u32[]{:S(2)}) async-start(bf16[16,4,4,4096]{3,2,1,0:T(4,128)(2,1)} %stack.15), calls=%async_computation.3 | async-start | bytes 4194304 | tf_op jit(solution)/shard_map/all_to_all | solution.py:54
  36.3 61.1 %all-gather.2.cloned.1.call-start = ((), (), s32[]{:S(2)}) async-start(), calls=%async_computation.5 | async-start | bytes 2228224 | tf_op jit(solution)/shard_map/all_gather | solution.py:50
  121.5 14.3 %copy-start = (bf16[4,64,4096]{2,0,1:T(4,128)(2,1)S(1)}, bf16[4,64,4096]{2,0,1:T(4,128)(2,1)}, u32[]{:S(2)}) copy-start(bf16[4,64,4096]{2,0,1:T(4,128)(2,1)} %all-gather.2.cloned.1.call-done) | copy-start | bytes 6291460
  344.5 11.9 %all-to-all-start.4 = ((bf16[2,8,4096]{2,1,0:T(8,128)(2,1)}), bf16[2,8,4096]{2,1,0:T(8,128)(2,1)S(1)}, u32[]{:S(2)}, u32[]{:S(2)}) async-start(bf16[2,8,4096]{2,1,0:T(8,128)(2,1)} %copy.83), calls=%async_computation.4 | async-start | bytes 262144 | tf_op jit(solution)/shard_map/all_to_all | solution.py:87
  347.9 16.0 %copy-start.2 = (f32[4,2]{0,1:T(2,128)S(1)}, f32[4,2]{0,1:T(2,128)}, u32[]{:S(2)}) copy-start(f32[4,2]{0,1:T(2,128)} %param.8) | copy-start | bytes 100
  356.5 7.4 %all-to-all-start.1 = ((bf16[2,8,4096]{2,1,0:T(8,128)(2,1)}), bf16[2,8,4096]{2,1,0:T(8,128)(2,1)S(1)}, u32[]{:S(2)}, u32[]{:S(2)}) async-start(bf16[2,8,4096]{2,1,0:T(8,128)(2,1)} %copy.73), calls=%async_computation.1 | async-start | bytes 262144 | tf_op jit(solution)/shard_map/all_to_all | solution.py:72
Sparse Core Ops, SparseCore 0:
  39.9 57.5 all-gather.1
